TPU v7x, 32 devices: a whole 2x2x4 slice. The times are simulated.
32 devices in a mesh: sample: 4 (over x, core), ctx: 8 (over z, y).
Axes of the slice: x: 2, y: 2, z: 4, core: 2. Of those that a mesh axis runs over, the one named last changes fastest.
Arguments:
- queries: bfloat16 [4096, 2048], P(('sample', 'ctx')), may hold values from -4 to 4
- experts: int32 [4096, 16], P(('sample', 'ctx')), may hold values from 0 to 63, all different within a row; in each aligned block of 128 rows (0 to 127, 128 to 255, ...) at most 64 rows name the same one
- gate: float32 [4096, 16], P(('sample', 'ctx')), may hold values from 0.05 to 1
- prefix_keys: bfloat16 [128, 1024], P('ctx'), may hold values from -8 to 8
- prefix_values: bfloat16 [128, 1024], P('ctx'), may hold values from -6 to 6
- d_out: bfloat16 [4096, 2048], P(('sample', 'ctx')), may hold values from -6 to 6
- lengths: int32 [4], replicated, may hold values from 128 to 1024
Outputs:
- attended: bfloat16 [4096, 2048], P(('sample', 'ctx'))
- query_grad: bfloat16 [4096, 2048], P(('sample', 'ctx'))
- gate_grad: float32 [4096, 16], P(('sample', 'ctx'))
- key_grad: float32 [128, 1024], P('ctx')
- value_grad: float32 [128, 1024], P('ctx')
Inputs may be any that keep to these rules, and one draw needn't show every extreme that they name: `experts`: among the tokens of one device (aligned blocks of 128 tokens) no expert is picked more than 64 times, and some expert is picked exactly 64 times; a token's picks are distinct. Completion c holds tokens c * 1024 to (c + 1) * 1024 - 1; its first lengths[c] tokens are live.
All inputs are finite; a program needn't handle non-finite values.
Results may differ from a plain program's by a relative error of at most 0.012.
Values may be sent and summed in bfloat16 or wider, within the bound.
No kernel may reach another device: no remote copies, remote signals or barrier semaphores. Data moves between devices by JAX's collectives and lax.ppermute only.
A program may use at most 64 MiB of HBM per device.

v0:
```python
import jax
import jax.numpy as jnp
from jax import lax
from jax.sharding import PartitionSpec as P

HEAD = 128
KV_HEADS = 8
EXPERTS = 64
TOPK = 16
CLEN = 1024
CAP = 64


def slot_index(experts):
    flat = experts.reshape(-1)
    picked = (flat[:, None] == jnp.arange(EXPERTS, dtype=jnp.int32)[None, :]).astype(jnp.int32)
    before = jnp.cumsum(picked, axis=0) - picked
    return flat * CAP + jnp.sum(before * picked, axis=1)


def over_blocks(step, carry, pieces, start):
    keys, values = pieces
    length = keys.shape[0]
    if length > 128 and length % 128 == 0:

        def inner(state, number):
            begin = number * 128
            key_block = lax.dynamic_slice_in_dim(keys, begin, 128, 0)
            value_block = lax.dynamic_slice_in_dim(values, begin, 128, 0)
            return (step(state, key_block, value_block, start + begin), None)

        carry, _ = lax.scan(inner, carry, jnp.arange(length // 128, dtype=jnp.int32))
        return carry
    return step(carry, keys, values, start)


def local(queries, experts, gate, prefix_keys, prefix_values, d_out, lengths):
    scale = HEAD ** (-0.5)
    width = KV_HEADS * HEAD
    group = EXPERTS * CAP // KV_HEADS
    rows = queries.shape[0]
    n_ctx = lax.axis_size("ctx")
    prefix_total = prefix_keys.shape[0] * n_ctx
    block = lax.axis_index("sample") * n_ctx + lax.axis_index("ctx")
    token_ids = block * rows + jnp.arange(rows, dtype=jnp.int32)
    owners = (token_ids // CLEN)[:, None] == jnp.arange(lengths.shape[0], dtype=jnp.int32)[None, :]
    chosen = jnp.sum(jnp.where(owners, lengths[None, :], 0), axis=1)
    live = (token_ids % CLEN < chosen).astype(jnp.float32)
    slots = slot_index(experts)
    q_buf = jnp.zeros((EXPERTS * CAP, HEAD), jnp.bfloat16).at[slots].set(queries.reshape(-1, HEAD))
    q_buf = q_buf.reshape(KV_HEADS, group, HEAD)

    def scores_of(key_block):
        heads = key_block.reshape(-1, KV_HEADS, HEAD)
        return jnp.einsum("hgd,phd->hgp", q_buf, heads, preferred_element_type=jnp.float32) * scale

    def forward_step(carry, key_block, value_block, start):
        high, total, accum = carry
        score = scores_of(key_block)
        new_high = jnp.maximum(high, jnp.max(score, axis=2))
        shrink = jnp.exp(high - new_high)
        weight = jnp.exp(score - new_high[..., None])
        total = total * shrink + jnp.sum(weight, axis=2)
        heads = value_block.reshape(-1, KV_HEADS, HEAD)
        accum = accum * shrink[..., None] + jnp.einsum(
            "hgp,phd->hgd", weight.astype(jnp.bfloat16), heads, preferred_element_type=jnp.float32
        )
        return (new_high, total, accum)

    start_state = (
        jnp.full((KV_HEADS, group), -1e30, jnp.float32),
        jnp.zeros((KV_HEADS, group), jnp.float32),
        jnp.zeros((KV_HEADS, group, HEAD), jnp.float32),
    )
    high, total, accum = over_blocks(
        forward_step,
        start_state,
        (
            lax.all_gather(prefix_keys, "ctx", axis=0, tiled=True),
            lax.all_gather(prefix_values, "ctx", axis=0, tiled=True),
        ),
        jnp.int32(0),
    )
    output = accum / total[..., None]
    lse = high + jnp.log(total)
    o_rows = output.reshape(EXPERTS * CAP, HEAD)[slots].reshape(rows, TOPK, HEAD)
    cot = d_out.astype(jnp.float32).reshape(rows, TOPK, HEAD)
    factor = gate * live[:, None]
    attended = (factor[..., None] * o_rows).reshape(rows, TOPK * HEAD).astype(jnp.bfloat16)
    gate_grad = live[:, None] * jnp.sum(o_rows * cot, axis=2)
    dout_rows = (factor[..., None] * cot).astype(jnp.bfloat16)
    dout_buf = (
        jnp.zeros((EXPERTS * CAP, HEAD), jnp.bfloat16).at[slots].set(dout_rows.reshape(-1, HEAD))
    )
    dout_buf = dout_buf.reshape(KV_HEADS, group, HEAD)
    delta = jnp.sum(dout_buf.astype(jnp.float32) * output, axis=2)

    def backward_step(carry, key_block, value_block, start):
        dq_accum, grads = carry
        key_heads = key_block.reshape(-1, KV_HEADS, HEAD)
        value_heads = value_block.reshape(-1, KV_HEADS, HEAD)
        prob = jnp.exp(scores_of(key_block) - lse[..., None])
        dprob = jnp.einsum(
            "hgd,phd->hgp", dout_buf, value_heads, preferred_element_type=jnp.float32
        )
        dscore = (prob * (dprob - delta[..., None])).astype(jnp.bfloat16)
        dq_accum = (
            dq_accum
            + jnp.einsum("hgp,phd->hgd", dscore, key_heads, preferred_element_type=jnp.float32)
            * scale
        )
        key_part = (
            jnp.einsum("hgp,hgd->phd", dscore, q_buf, preferred_element_type=jnp.float32) * scale
        )
        value_part = jnp.einsum(
            "hgp,hgd->phd", prob.astype(jnp.bfloat16), dout_buf, preferred_element_type=jnp.float32
        )
        joined = jnp.concatenate(
            [key_part.reshape(-1, width), value_part.reshape(-1, width)], axis=1
        )
        grads = lax.dynamic_update_slice_in_dim(grads, joined, start, 0)
        return (dq_accum, grads)

    back_state = (
        jnp.zeros((KV_HEADS, group, HEAD), jnp.float32),
        jnp.zeros((prefix_total, 2 * width), jnp.float32),
    )
    dq_buf, grads = over_blocks(
        backward_step,
        back_state,
        (
            lax.all_gather(prefix_keys, "ctx", axis=0, tiled=True),
            lax.all_gather(prefix_values, "ctx", axis=0, tiled=True),
        ),
        jnp.int32(0),
    )
    query_grad = (
        dq_buf.reshape(EXPERTS * CAP, HEAD)[slots].reshape(rows, TOPK * HEAD).astype(jnp.bfloat16)
    )
    share = lax.psum_scatter(grads, "ctx", scatter_dimension=0, tiled=True)
    summed = lax.psum(share, "sample")
    return (attended, query_grad, gate_grad, summed[:, :width], summed[:, width:])


def solution(mesh):
    placed = (
        P(("sample", "ctx"), None),
        P(("sample", "ctx"), None),
        P(("sample", "ctx"), None),
        P("ctx", None),
        P("ctx", None),
        P(("sample", "ctx"), None),
        P(),
    )
    return jax.shard_map(
        local,
        mesh=mesh,
        in_specs=placed,
        out_specs=(
            P(("sample", "ctx"), None),
            P(("sample", "ctx"), None),
            P(("sample", "ctx"), None),
            P("ctx", None),
            P("ctx", None),
        ),
        check_vma=False,
    )
```

profile of v0, /device:TPU:0, one launch (start us, length us, event | category | flops | bytes accessed | tf_op | source)
XLA Modules:
  0.0 241.1 jit_solution(4302260018361914511)
XLA Ops:
  7.9 0.8 copy.73
  8.9 0.7 select_reduce_fusion
  10.4 1.4 copy.71
  11.8 32.8 %all_gather.8 = bf16[128,1024]{1,0:T(8,128)(2,1)S(1)} all-gather(bf16[16,1024]{1,0:T(8,128)(2,1)} %param.10), channel_id=1, replica_groups=mesh['sample'=4,'ctx'=8] {'ctx'}, dimensions={0}, use_global_device_ids=true | all-gather | bytes 294912 | tf_op jit(solution)/shard_map/all_gather | solution.py:79
  44.7 31.0 %all_gather.9 = bf16[128,1024]{1,0:T(8,128)(2,1)S(1)} all-gather(bf16[16,1024]{1,0:T(8,128)(2,1)} %param.11), channel_id=1, replica_groups=mesh['sample'=4,'ctx'=8] {'ctx'}, dimensions={0}, use_global_device_ids=true | all-gather | bytes 294912 | tf_op jit(solution)/shard_map/all_gather | solution.py:80
  75.7 0.8 copy.79
  76.6 18.1 %reduce-window.6 = s32[64,16,128]{2,1,0:T(8,128)S(1)} reduce-window(s32[64,16,128]{2,1,0:T(8,128)S(1)} %fusion.17, s32[]{:T(128)} %constant.50.clone.1), window={size=1x1x128 pad=0_0x0_0x127_0}, to_apply=%region_1.2 | reduce-window | flops 16646144 | bytes 1048580 | tf_op jit(solution)/shard_map/reduce-window
  96.1 1.0 reshape.198
  97.4 6.6 %scatter_custom_fusion = bf16[4096,128]{1,0:T(8,128)(2,1)S(1)} fusion(s32[2048]{0:T(1024)S(1)} %bitcast.70, bf16[2048,128]{1,0:T(8,128)(2,1)} %reshape.198, bf16[]{:T(256)} %constant.57.clone.1), kind=kCustom, calls=%fused_computation.32 | custom fusion | bytes 1049088 | tf_op jit(solution)/shard_map/scatter | solution.py:50
  105.1 2.3 add_divide_fusion
  107.4 7.6 %gather_fusion = f32[2048,128]{1,0:T(8,128)} fusion(f32[4096,128]{1,0:T(8,128)S(1)} %bitcast.51, s32[2048]{0:T(1024)S(1)} %broadcast_clamp_fusion), kind=kCustom, calls=%fused_computation | custom fusion | bytes 2105344 | tf_op jit(solution)/shard_map/gather | solution.py:86
  115.0 1.6 multiply_reduce_fusion.1
  116.6 0.9 broadcast_multiply_fusion
  118.2 7.4 %scatter_custom_fusion.1 = bf16[4096,128]{1,0:T(8,128)(2,1)S(1)} fusion(s32[2048]{0:T(1024)} %bitcast.71, f32[2048,128]{1,0:T(8,128)} %copy-done.2, f32[2048]{0:T(1024)} %mul.105, bf16[]{:T(256)} %constant.57.clone.1), kind=kCustom, calls=%fused_computation.23 | custom fusion | flops 524288 | bytes 2105856 | tf_op jit(solution)/shard_map/scatter | solution.py:93
  126.3 0.9 copy-done.1
  127.2 1.4 fusion.3
  130.4 1.0 copy.92
  131.6 2.2 pad_maximum_fusion
  134.4 1.2 fusion.6
  135.6 64.0 %reduce-scatter.2.cloned.1.call-done = f32[16,2048]{1,0:T(8,128)} async-done(((f32[128,2048]{1,0:T(8,128)}), f32[16,2048]{1,0:T(8,128)}) %reduce-scatter.2.cloned.1.call-update) | async-done | bytes 131088 | tf_op jit(solution)/shard_map/reduce_scatter | solution.py:140
  201.4 6.2 %gather_fusion.1 = bf16[2048,128]{1,0:T(8,128)(2,1)S(1)} fusion(bf16[4096,128]{1,0:T(8,128)(2,1)S(1)} %bitcast.52, s32[2048]{0:T(1024)S(1)} %copy-done.12), kind=kCustom, calls=%fused_computation.1 | custom fusion | bytes 1056768 | tf_op jit(solution)/shard_map/gather | solution.py:138
  207.6 1.0 convert_element_type.49
  208.6 24.1 %all-reduce.2.cloned.1.call-done = f32[16,2048]{1,0:T(8,128)} async-done(((f32[16,2048]{1,0:T(8,128)}), f32[16,2048]{1,0:T(8,128)}) %all-reduce.2.cloned.1.call-update) | async-done | bytes 131088 | tf_op jit(solution)/shard_map/psum | solution.py:141
  232.7 1.5 fusion.19
  (63 shorter events, 10.2 us)
Async XLA Ops:
  7.2 192.4 %reduce-scatter.2.cloned.1.call-start = ((), (), s32[]{:S(2)}) async-start(), calls=%async_computation.1 | async-start | bytes 1179648 | tf_op jit(solution)/shard_map/reduce_scatter | solution.py:140
  76.6 19.5 %copy-start.10 = (bf16[128,2048]{1,0:T(8,128)(2,1)S(1)}, bf16[128,2048]{1,0:T(8,128)(2,1)}, u32[]{:S(2)}) copy-start(bf16[128,2048]{1,0:T(8,128)(2,1)} %param.7) | copy-start | bytes 1572868
  94.7 2.4 %copy-start.9 = (bf16[128,2048]{1,0:T(8,128)(2,1)S(1)}, bf16[128,2048]{1,0:T(8,128)(2,1)}, u32[]{:S(2)}) copy-start(bf16[128,2048]{1,0:T(8,128)(2,1)} %param.12) | copy-start | bytes 1572868
  96.1 7.9 %copy-start.13 = (s32[2048,1]{0,1:T(1,128)}, s32[2048,1]{0,1:T(1,128)S(1)}, u32[]{:S(2)}) copy-start(s32[2048,1]{0,1:T(1,128)S(1)} %compare_select_fusion) | copy-start | bytes 24580
  96.1 11.3 %copy-start.11 = (s32[2048]{0:T(1024)}, s32[2048]{0:T(1024)S(1)}, u32[]{:S(2)}) copy-start(s32[2048]{0:T(1024)S(1)} %broadcast_clamp_fusion) | copy-start | bytes 24580
  97.3 17.6 %copy-start.2 = (f32[2048,128]{1,0:T(8,128)}, f32[2048,128]{1,0:T(8,128)S(1)}, u32[]{:S(2)}) copy-start(f32[2048,128]{1,0:T(8,128)S(1)} %reshape.177) | copy-start | bytes 3145732
  103.9 1.0 copy-start.3
  104.0 1.2 copy-start.7
  104.5 2.9 %copy-start = (f32[8,512,128]{1,2,0:T(8,128)}, f32[8,512,128]{1,2,0:T(8,128)S(1)}, u32[]{:S(2)}) copy-start(f32[8,512,128]{1,2,0:T(8,128)S(1)} %get-tuple-element.28) | copy-start | bytes 6291460
  125.6 1.6 copy-start.1
  126.3 2.4 copy-start.8
  128.7 1.2 copy-start.4
  129.9 1.5 copy-start.6
  131.4 2.5 %copy-start.5 = (f32[2048,128]{1,0:T(8,128)S(1)}, f32[2048,128]{1,0:T(8,128)}, u32[]{:S(2)}) copy-start(f32[2048,128]{1,0:T(8,128)} %gather_fusion) | copy-start | bytes 3145732
  133.9 98.9 %all-reduce.2.cloned.1.call-start = ((), (), s32[]{:S(2)}) async-start(), calls=%async_computation.2 | async-start | bytes 262144 | tf_op jit(solution)/shard_map/psum | solution.py:141
  199.6 1.8 copy-start.12
Sparse Core Ops, SparseCore 0:
  134.0 65.5 reduce-scatter.1
  201.9 30.7 all-reduce.1
where the time goes:
time: 242 us; the launch traced here: 241 us
  waiting for transfers between devices  88.2 us (36%)
  blocking collectives  63.7 us (26%)
  other arithmetic  35.1 us (15%)
  local copies, waits for them, and re-layouts  34 us (14%)
  between operations  14.4 us (6%)
  matrix products  5.69 us (2%)
    reduce_scatter x1, waiting for transfers between devices, local(): share = lax.psum_scatter(grads, 'ctx', scatter_dimension=0, tiled=True)  64 us
    all_gather x1, blocking collectives, local(): lax.all_gather(prefix_keys, 'ctx', axis=0, tiled=True)  32.8 us
    all_gather x1, blocking collectives, local(): lax.all_gather(prefix_values, 'ctx', axis=0, tiled=True)  31 us
    psum x1, waiting for transfers between devices, local(): summed = lax.psum(share, 'sample')  24.1 us
    another operation x3, other arithmetic  18.5 us
    gather x1, local copies, waits for them, and re-layouts, local(): output.reshape(EXPERTS * CAP, HEAD)[slots].reshape(rows, TOPK, HEAD)  7.56 us
    scatter x1, other arithmetic, local(): jnp.zeros((EXPERTS * CAP, HEAD), jnp.bfloat16).at[slots]  7.39 us
    scatter x1, local copies, waits for them, and re-layouts, local(): jnp.zeros((EXPERTS * CAP, HEAD), jnp.bfloat16).at[slots]  6.57 us
  transfers between devices with their start and end apart: 2, of which 2 were waited for; matrix products, arithmetic and copies ran while one was open for 4% of the time, Pallas kernels for 0%

commit v1 on v0

--- a/solution.py
+++ b/solution.py
@@ -138,7 +138,8 @@
         dq_buf.reshape(EXPERTS * CAP, HEAD)[slots].reshape(rows, TOPK * HEAD).astype(jnp.bfloat16)
     )
     share = lax.psum_scatter(grads, "ctx", scatter_dimension=0, tiled=True)
-    summed = lax.psum(share, "sample")
+    parts = lax.all_gather(share, "sample")
+    summed = jnp.sum(parts, axis=0)
     return (attended, query_grad, gate_grad, summed[:, :width], summed[:, width:])
 
 

time: 242 us -> 214 us (0.88)
  waiting for transfers between devices: 88.2 us -> 54.5 us
  blocking collectives: 63.7 us -> 71.1 us
    psum x1 -> x0, waiting for transfers between devices: 24.1 us -> none  [local(): summed = lax.psum(share, 'sample')]
    reduce_scatter x1, waiting for transfers between devices: 64 us -> 54.5 us  [local(): share = lax.psum_scatter(grads, 'ctx', scatter_dimension=0, tiled=True)]
    all_gather x0 -> x1, blocking collectives: none -> 7.34 us  [local(): parts = lax.all_gather(share, 'sample')]
  transfers between devices with their start and end apart: 2 -> 1, of which waited for: 2 -> 1; matrix products, arithmetic and copies ran while one was open for 4% -> 5% of each run, Pallas kernels for 0% -> 0%
where the time goes in v1:
time: 214 us
  blocking collectives  71.1 us (33%)
  waiting for transfers between devices  54.5 us (25%)
  other arithmetic  35.8 us (17%)
  local copies, waits for them, and re-layouts  32.5 us (15%)
  between operations  14.3 us (7%)
  matrix products  5.69 us (3%)
    reduce_scatter x1, waiting for transfers between devices, local(): share = lax.psum_scatter(grads, 'ctx', scatter_dimension=0, tiled=True)  54.5 us
    all_gather x1, blocking collectives, local(): lax.all_gather(prefix_keys, 'ctx', axis=0, tiled=True)  32.8 us
    all_gather x1, blocking collectives, local(): lax.all_gather(prefix_values, 'ctx', axis=0, tiled=True)  31 us
    another operation x3, other arithmetic  18.5 us
    scatter x1, other arithmetic, local(): jnp.zeros((EXPERTS * CAP, HEAD), jnp.bfloat16).at[slots]  7.62 us
    gather x1, local copies, waits for them, and re-layouts, local(): output.reshape(EXPERTS * CAP, HEAD)[slots].reshape(rows, TOPK, HEAD)  7.56 us
    all_gather x1, blocking collectives, local(): parts = lax.all_gather(share, 'sample')  7.34 us
    scatter x1, local copies, waits for them, and re-layouts, local(): jnp.zeros((EXPERTS * CAP, HEAD), jnp.bfloat16).at[slots]  6.57 us
  transfers between devices with their start and end apart: 1, of which 1 were waited for; matrix products, arithmetic and copies ran while one was open for 5% of the time, Pallas kernels for 0%

profile of v1, /device:TPU:0, one launch (start us, length us, event | category | flops | bytes accessed | tf_op | source)
XLA Modules:
  0.0 213.9 jit_solution(6854697959179428661)
XLA Ops:
  7.2 0.7 broadcast_multiply_fusion.2
  7.9 0.8 copy.71
  8.9 0.7 select_reduce_fusion
  10.4 0.8 copy.69
  11.2 32.8 %all_gather.14 = bf16[128,1024]{1,0:T(8,128)(2,1)S(1)} all-gather(bf16[16,1024]{1,0:T(8,128)(2,1)} %param.10), channel_id=1, replica_groups=mesh['sample'=4,'ctx'=8] {'ctx'}, dimensions={0}, use_global_device_ids=true | all-gather | bytes 294912 | tf_op jit(solution)/shard_map/all_gather | solution.py:79
  44.1 31.0 %all_gather.15 = bf16[128,1024]{1,0:T(8,128)(2,1)S(1)} all-gather(bf16[16,1024]{1,0:T(8,128)(2,1)} %param.11), channel_id=1, replica_groups=mesh['sample'=4,'ctx'=8] {'ctx'}, dimensions={0}, use_global_device_ids=true | all-gather | bytes 294912 | tf_op jit(solution)/shard_map/all_gather | solution.py:80
  75.1 0.8 copy.77
  76.0 18.1 %reduce-window.6 = s32[64,16,128]{2,1,0:T(8,128)S(1)} reduce-window(s32[64,16,128]{2,1,0:T(8,128)S(1)} %fusion.17, s32[]{:T(128)} %constant.50.clone.1), window={size=1x1x128 pad=0_0x0_0x127_0}, to_apply=%region_1.2 | reduce-window | flops 16646144 | bytes 1048580 | tf_op jit(solution)/shard_map/reduce-window
  95.5 1.0 reshape.198
  96.7 6.6 %scatter_custom_fusion = bf16[4096,128]{1,0:T(8,128)(2,1)S(1)} fusion(s32[2048]{0:T(1024)S(1)} %bitcast.72, bf16[2048,128]{1,0:T(8,128)(2,1)} %reshape.198, bf16[]{:T(256)} %constant.57.clone.1), kind=kCustom, calls=%fused_computation.32 | custom fusion | bytes 1049088 | tf_op jit(solution)/shard_map/scatter | solution.py:50
  104.5 2.3 %add_divide_fusion = f32[8,512,128]{2,1,0:T(8,128)S(1)} fusion(bf16[128,8,128]{0,2,1:T(8,128)(2,1)S(1)} %bitcast.66, f32[8,512,128]{1,2,0:T(8,128)S(1)} %get-tuple-element.28, f32[8,512]{1,0:T(8,128)S(1)} %get-tuple-element.23, f32[8,512]{1,0:T(8,128)S(1)} %broadcast_maximum_fusion, f32[8,512]{1,0:T(8,128)S(1)} %get-tuple-element.24), kind=kOutput, calls=%fused_computation.7 | convolution fusion | flops 136314880 | bytes 4505600 | tf_op jit(solution)/shard_map/hgp,phd->hgd/dot_general | solution.py:65
  106.8 7.6 %gather_fusion = f32[2048,128]{1,0:T(8,128)} fusion(f32[4096,128]{1,0:T(8,128)S(1)} %bitcast.52, s32[2048]{0:T(1024)S(1)} %broadcast_clamp_fusion), kind=kCustom, calls=%fused_computation | custom fusion | bytes 2105344 | tf_op jit(solution)/shard_map/gather | solution.py:86
  114.4 1.6 multiply_reduce_fusion.1
  116.0 1.3 broadcast_multiply_fusion
  117.4 7.6 %scatter_custom_fusion.1 = bf16[4096,128]{1,0:T(8,128)(2,1)S(1)} fusion(s32[2048]{0:T(1024)} %bitcast.73, f32[2048,128]{1,0:T(8,128)} %copy-done.2, f32[2048]{0:T(1024)S(1)} %mul.105, bf16[]{:T(256)} %constant.57.clone.1), kind=kCustom, calls=%fused_computation.23 | custom fusion | flops 524288 | bytes 2105856 | tf_op jit(solution)/shard_map/scatter | solution.py:93
  125.7 0.9 copy-done.1
  126.7 1.4 fusion.3
  129.8 1.0 copy.90
  131.0 2.2 %pad_maximum_fusion = f32[128,2048]{1,0:T(8,128)} fusion(f32[128,1024]{1,0:T(8,128)S(1)} %copy.91, f32[128,1024]{1,0:T(8,128)} %copy.90), kind=kLoop, calls=%fused_computation.18 | loop fusion | flops 262144 | bytes 2097152 | tf_op jit(solution)/shard_map/concatenate | solution.py:118
  135.9 6.2 %gather_fusion.1 = bf16[2048,128]{1,0:T(8,128)(2,1)S(1)} fusion(bf16[4096,128]{1,0:T(8,128)(2,1)S(1)} %bitcast.53, s32[2048]{0:T(1024)S(1)} %copy-done.13), kind=kCustom, calls=%fused_computation.1 | custom fusion | bytes 1056768 | tf_op jit(solution)/shard_map/gather | solution.py:138
  142.1 1.0 convert_element_type.49
  143.4 1.2 fusion.6
  144.6 54.5 %reduce-scatter.2.cloned.1.call-done = f32[16,2048]{1,0:T(8,128)} async-done(((f32[128,2048]{1,0:T(8,128)}), f32[16,2048]{1,0:T(8,128)}) %reduce-scatter.2.cloned.1.call-update) | async-done | bytes 131088 | tf_op jit(solution)/shard_map/reduce_scatter | solution.py:140
  199.0 7.3 %all-gather = f32[64,2048]{1,0:T(8,128)S(1)} all-gather(f32[16,2048]{1,0:T(8,128)} %reduce-scatter.2.cloned.1.call-done), channel_id=2, replica_groups=mesh['sample'=4,'ctx'=8] {'sample'}, dimensions={0}, use_global_device_ids=true | all-gather | bytes 655360 | tf_op jit(solution)/shard_map/all_gather | solution.py:141
  (64 shorter events, 10.1 us)
Async XLA Ops:
  7.2 191.9 %reduce-scatter.2.cloned.1.call-start = ((), (), s32[]{:S(2)}) async-start(), calls=%async_computation.1 | async-start | bytes 1179648 | tf_op jit(solution)/shard_map/reduce_scatter | solution.py:140
  76.0 19.5 %copy-start.10 = (bf16[128,2048]{1,0:T(8,128)(2,1)S(1)}, bf16[128,2048]{1,0:T(8,128)(2,1)}, u32[]{:S(2)}) copy-start(bf16[128,2048]{1,0:T(8,128)(2,1)} %param.7) | copy-start | bytes 1572868
  94.1 2.4 %copy-start.9 = (bf16[128,2048]{1,0:T(8,128)(2,1)S(1)}, bf16[128,2048]{1,0:T(8,128)(2,1)}, u32[]{:S(2)}) copy-start(bf16[128,2048]{1,0:T(8,128)(2,1)} %param.12) | copy-start | bytes 1572868
  95.4 7.9 %copy-start.14 = (s32[2048,1]{0,1:T(1,128)}, s32[2048,1]{0,1:T(1,128)S(1)}, u32[]{:S(2)}) copy-start(s32[2048,1]{0,1:T(1,128)S(1)} %compare_select_fusion) | copy-start | bytes 24580
  95.5 11.3 %copy-start.12 = (s32[2048]{0:T(1024)}, s32[2048]{0:T(1024)S(1)}, u32[]{:S(2)}) copy-start(s32[2048]{0:T(1024)S(1)} %broadcast_clamp_fusion) | copy-start | bytes 24580
  96.7 17.6 %copy-start.2 = (f32[2048,128]{1,0:T(8,128)}, f32[2048,128]{1,0:T(8,128)S(1)}, u32[]{:S(2)}) copy-start(f32[2048,128]{1,0:T(8,128)S(1)} %reshape.177) | copy-start | bytes 3145732
  103.3 1.0 copy-start.3
  103.3 1.2 copy-start.7
  103.8 2.9 %copy-start = (f32[8,512,128]{1,2,0:T(8,128)}, f32[8,512,128]{1,2,0:T(8,128)S(1)}, u32[]{:S(2)}) copy-start(f32[8,512,128]{1,2,0:T(8,128)S(1)} %get-tuple-element.28) | copy-start | bytes 6291460
  125.1 1.6 copy-start.1
  125.7 2.4 %copy-start.8 = (bf16[128,1024]{0,1:T(8,128)(2,1)S(1)}, bf16[128,1024]{0,1:T(8,128)(2,1)}, u32[]{:S(2)}) copy-start(bf16[128,1024]{0,1:T(8,128)(2,1)} %copy.77) | copy-start | bytes 786436
  128.1 1.2 copy-start.4
  129.3 1.5 copy-start.6
  130.8 2.5 %copy-start.5 = (f32[2048,128]{1,0:T(8,128)S(1)}, f32[2048,128]{1,0:T(8,128)}, u32[]{:S(2)}) copy-start(f32[2048,128]{1,0:T(8,128)} %gather_fusion) | copy-start | bytes 3145732
  133.3 0.8 copy-start.11
  134.8 1.1 copy-start.13
Sparse Core Ops, SparseCore 0:
  133.4 65.5 reduce-scatter.1
